TPU v7x, 32 devices: a whole 2x2x4 slice. The times are simulated.
32 devices in a mesh: shard: 4 (over y, x), ctx: 2 (over core), tp: 4 (over z).
Axes of the slice: x: 2, y: 2, z: 4, core: 2. Of those that a mesh axis runs over, the one named last changes fastest.
Arguments:
- tokens: bfloat16 [4, 1024, 1536], P('shard', ('ctx', 'tp')), may hold values from -6 to 6
- cotangent: bfloat16 [4, 1024, 1536], P('shard', ('ctx', 'tp')), may hold values from -6 to 6
- lengths: int32 [4], P('shard'), may hold values from 256 to 1024, as said below
- w_qkv: bfloat16 [1536, 3, 1536], P(('shard', 'ctx'), None, 'tp'), may hold values from -0.15625 to 0.15625
- w_forget: bfloat16 [1536, 24], P(('shard', 'ctx'), 'tp'), may hold values from -0.15625 to 0.15625
- forget_bias: float32 [24], replicated, may hold values from 3 to 8
- w_ogate: bfloat16 [1536, 1536], P(('shard', 'ctx'), 'tp'), may hold values from -0.15625 to 0.15625
- w_out: bfloat16 [1536, 1536], P(('shard', 'ctx'), 'tp'), may hold values from -0.625 to 0.625
- w_gu: bfloat16 [1536, 2, 4096], P(('shard', 'ctx'), None, 'tp'), may hold values from -0.15625 to 0.15625
- w_down: bfloat16 [1536, 4096], P(('shard', 'ctx'), 'tp'), may hold values from -0.09375 to 0.09375
- gain_attn: float32 [1536], replicated, may hold values from 0.5 to 1.5
- gain_mlp: float32 [1536], replicated, may hold values from 0.5 to 1.5
- qk_gain: float32 [2, 64], replicated, may hold values from 1 to 2
Outputs:
- output: bfloat16 [4, 1024, 1536], P('shard', ('ctx', 'tp'))
- input_grad: bfloat16 [4, 1024, 1536], P('shard', ('ctx', 'tp'))
- grad_qkv: float32 [1536, 3, 1536], P(('shard', 'ctx'), None, 'tp')
- grad_forget: float32 [1536, 24], P(('shard', 'ctx'), 'tp')
- grad_forget_bias: float32 [24], replicated
- grad_ogate: float32 [1536, 1536], P(('shard', 'ctx'), 'tp')
- grad_out: float32 [1536, 1536], P(('shard', 'ctx'), 'tp')
- grad_gu: float32 [1536, 2, 4096], P(('shard', 'ctx'), None, 'tp')
- grad_down: float32 [1536, 4096], P(('shard', 'ctx'), 'tp')
- grad_gain_attn: float32 [1536], replicated
- grad_gain_mlp: float32 [1536], replicated
- grad_qk_gain: float32 [2, 64], replicated
Inputs may be any that keep to these rules, and one draw needn't show every extreme that they name: `lengths`: real tokens of a slot; positions at or past it are padding; both the least and the most value occur in every draw.
All inputs are finite; a program needn't handle non-finite values.
Results may differ from a plain program's by a relative error of at most 0.04.
Values may be sent and summed in bfloat16 or wider, within the bound.
No kernel may reach another device: no remote copies, remote signals or barrier semaphores. Data moves between devices by JAX's collectives and lax.ppermute only.
A program may use at most 128 MiB of HBM per device.

v0:
```python
import math
import jax
import jax.numpy as jnp
from jax import lax
from jax.sharding import PartitionSpec as P

epsilon = 1e-06


def shifted(block, axis, distance):
    devices = range(lax.axis_size(axis))
    route = [(i - distance, i) for i in devices if i - distance in devices]
    return lax.ppermute(block, axis, route)


def norm_rows(values, gain):
    return values * lax.rsqrt(jnp.mean(values * values, axis=-1, keepdims=True) + epsilon) * gain


def product(left, right):
    return jnp.dot(left, right, preferred_element_type=jnp.float32)


def product_t(left, right):
    return lax.dot_general(
        left, right, (((1,), (1,)), ((), ())), preferred_element_type=jnp.float32
    )


def outer_rows(left, right):
    return lax.dot_general(
        left, right, (((0,), (0,)), ((), ())), preferred_element_type=jnp.float32
    )


def body(
    tokens,
    cotangent,
    lengths,
    w_qkv,
    w_forget,
    forget_bias,
    w_ogate,
    w_out,
    w_gu,
    w_down,
    gain_attn,
    gain_mlp,
    qk_gain,
):
    slot_count, own_rows, model_width = tokens.shape
    tensor_size = lax.axis_size("tp")
    tensor_place = lax.axis_index("tp")
    span_index = lax.axis_index("ctx")
    half_rows = own_rows * tensor_size
    row_count = slot_count * half_rows
    local_heads = w_forget.shape[1]
    head_size = qk_gain.shape[1]
    head_cols = local_heads * head_size
    hidden_units = w_down.shape[1]
    item_count = slot_count * local_heads
    score_scale = 1.0 / math.sqrt(head_size)
    own_start = tensor_place * own_rows
    full_tokens, full_cot = (
        lax.all_gather(tokens, "tp", axis=1, tiled=True),
        lax.all_gather(cotangent, "tp", axis=1, tiled=True),
    )
    qkv_full, forget_full, ogate_full, out_full, gu_full, down_full = (
        lax.all_gather(w_qkv, ("shard", "ctx"), axis=0, tiled=True),
        lax.all_gather(w_forget, ("shard", "ctx"), axis=0, tiled=True),
        lax.all_gather(w_ogate, ("shard", "ctx"), axis=0, tiled=True),
        lax.all_gather(w_out, ("shard", "ctx"), axis=0, tiled=True),
        lax.all_gather(w_gu, ("shard", "ctx"), axis=0, tiled=True),
        lax.all_gather(w_down, ("shard", "ctx"), axis=0, tiled=True),
    )
    qkv_flat = qkv_full.reshape(model_width, 3 * head_cols)
    gu_flat = gu_full.reshape(model_width, 2 * hidden_units)

    def own_slice(values):
        return lax.dynamic_slice_in_dim(
            values.reshape(slot_count, half_rows, values.shape[-1]), own_start, own_rows, 1
        )

    positions = span_index * half_rows + jnp.arange(half_rows, dtype=jnp.int32)
    valid_rows = (positions[None, :] < lengths[:, None]).astype(jnp.float32).reshape(row_count, 1)
    own_positions = span_index * half_rows + own_start + jnp.arange(own_rows, dtype=jnp.int32)
    valid_own = (own_positions[None, :] < lengths[:, None]).astype(jnp.float32)[:, :, None]
    residual = full_tokens.reshape(row_count, model_width).astype(jnp.float32)
    normed = norm_rows(residual, gain_attn).astype(jnp.bfloat16)
    qkv_rows = product(normed, qkv_flat).reshape(row_count, 3, head_cols)
    query_raw = qkv_rows[:, 0].reshape(row_count, local_heads, head_size)
    key_raw = qkv_rows[:, 1].reshape(row_count, local_heads, head_size)
    queries = (
        norm_rows(query_raw, qk_gain[0])
        .astype(jnp.bfloat16)
        .reshape(slot_count, half_rows, head_cols)
    )
    keys_here = (
        norm_rows(key_raw, qk_gain[1])
        .astype(jnp.bfloat16)
        .reshape(slot_count, half_rows, head_cols)
    )
    values_here = qkv_rows[:, 2].astype(jnp.bfloat16).reshape(slot_count, half_rows, head_cols)
    bias_here = lax.dynamic_slice_in_dim(forget_bias, tensor_place * local_heads, local_heads)
    forget_pre = (product(normed, forget_full) + bias_here).reshape(
        slot_count, half_rows, local_heads
    )
    cum_here = jnp.cumsum(jax.nn.log_sigmoid(forget_pre), axis=1)
    keys_left, values_left = shifted((keys_here, values_here), "ctx", 1)
    cum_left = shifted(cum_here, "ctx", 1)
    cum_query = cum_here + cum_left[:, -1:, :]

    def by_head(values):
        shaped = values.reshape(slot_count, half_rows, local_heads, head_size)
        return jnp.transpose(shaped, (0, 2, 1, 3)).reshape(item_count, half_rows, head_size)

    def by_head_cum(values):
        return jnp.transpose(values, (0, 2, 1)).reshape(item_count, half_rows)

    def to_slots(values):
        shaped = values.reshape(slot_count, local_heads, half_rows, head_size)
        return jnp.transpose(shaped, (0, 2, 1, 3)).reshape(slot_count, half_rows, head_cols)

    def to_slots_cum(values):
        return jnp.transpose(values.reshape(slot_count, local_heads, half_rows), (0, 2, 1))

    q_items = by_head(queries)
    k_items = jnp.concatenate([by_head(keys_left), by_head(keys_here)], axis=1)
    v_items = jnp.concatenate([by_head(values_left), by_head(values_here)], axis=1)
    cq_items = by_head_cum(cum_query)
    ck_items = jnp.concatenate([by_head_cum(cum_left), cq_items], axis=1)
    place_ids = jnp.arange(half_rows, dtype=jnp.int32)
    earlier = jnp.broadcast_to(span_index > 0, (half_rows, half_rows))
    allowed = jnp.concatenate([earlier, place_ids[None, :] <= place_ids[:, None]], axis=1)

    def score_block(query_block, key_block, cum_rows, cum_cols):
        score_raw = (
            product_t(query_block, key_block) * score_scale + cum_rows[:, None] - cum_cols[None, :]
        )
        return jnp.where(allowed, score_raw, -jnp.inf)

    def forward_item(pieces):
        query_block, key_block, value_block, cum_rows, cum_cols = pieces
        score_vals = score_block(query_block, key_block, cum_rows, cum_cols)
        row_max = jnp.max(score_vals, axis=1, keepdims=True)
        expo = jnp.exp(score_vals - row_max)
        row_total = jnp.sum(expo, axis=1, keepdims=True)
        attn_probs = (expo / row_total).astype(jnp.bfloat16)
        return (product(attn_probs, value_block), (row_max + jnp.log(row_total))[:, 0])

    attended_items, lse_items = lax.map(
        forward_item, (q_items, k_items, v_items, cq_items, ck_items)
    )
    attended_rows = to_slots(attended_items).reshape(row_count, head_cols)
    opener = jax.nn.sigmoid(product(normed, ogate_full))
    gated = (attended_rows * opener).astype(jnp.bfloat16)
    branch_part = product_t(gated, out_full)
    branch_full = lax.psum(branch_part, "tp")
    middle = residual + branch_full
    middle_share = own_slice(middle)
    normed_mid = norm_rows(middle, gain_mlp).astype(jnp.bfloat16)
    both = product(normed_mid, gu_flat).reshape(row_count, 2, hidden_units)
    gate_pre = both[:, 0]
    up_pre = both[:, 1]
    gate_sig = jax.nn.sigmoid(gate_pre)
    hidden = (gate_pre * gate_sig * up_pre).astype(jnp.bfloat16)
    down_share = lax.psum_scatter(
        product_t(hidden, down_full)
        .reshape(slot_count, half_rows, model_width)
        .astype(jnp.bfloat16),
        "tp",
        scatter_dimension=1,
        tiled=True,
    ).astype(jnp.float32)
    output = (valid_own * (middle_share + down_share)).astype(jnp.bfloat16)
    cot_rows = full_cot.reshape(row_count, model_width) * valid_rows.astype(jnp.bfloat16)
    d_hidden = product(cot_rows, down_full)
    d_gate = d_hidden * up_pre * gate_sig * (1.0 + gate_pre * (1.0 - gate_sig))
    d_up = d_hidden * gate_pre * gate_sig
    d_both = (
        jnp.stack([d_gate, d_up], axis=1).astype(jnp.bfloat16).reshape(row_count, 2 * hidden_units)
    )
    grad_down = outer_rows(cot_rows, hidden)
    grad_gu = outer_rows(normed_mid, d_both).reshape(model_width, 2, hidden_units)
    d_mid_terms = product_t(d_both, gu_flat)
    d_normed_mid = lax.psum(d_mid_terms, "tp")
    _, pull_mid = jax.vjp(norm_rows, middle, gain_mlp)
    d_middle_norm, d_gain_mlp_all = pull_mid(d_normed_mid)
    d_middle = d_middle_norm + cot_rows.astype(jnp.float32)
    feat_share = model_width // tensor_size
    owner = jnp.arange(model_width, dtype=jnp.int32) // feat_share == tensor_place
    d_gain_mlp_own = jnp.where(owner, d_gain_mlp_all, 0.0)
    d_branch = d_middle.astype(jnp.bfloat16)
    d_middle_share = own_slice(d_middle)
    d_gated = product(d_branch, out_full)
    grad_out = outer_rows(d_branch, gated)
    d_attended = (d_gated * opener).astype(jnp.bfloat16)
    d_open = (d_gated * attended_rows * opener * (1.0 - opener)).astype(jnp.bfloat16)
    grad_ogate = outer_rows(normed, d_open)
    da_items = by_head(d_attended.reshape(slot_count, half_rows, head_cols))

    def backward_item(pieces):
        query_block, key_block, value_block, cum_rows, cum_cols, lse_block, grad_block = pieces
        score_vals = score_block(query_block, key_block, cum_rows, cum_cols)
        attn_probs = jnp.exp(score_vals - lse_block[:, None])
        d_probs = product_t(grad_block, value_block)
        centre = jnp.sum(attn_probs * d_probs, axis=1, keepdims=True)
        d_scores = (attn_probs * (d_probs - centre)).astype(jnp.bfloat16)
        d_query_block = product(d_scores, key_block) * score_scale
        d_key_block = outer_rows(d_scores, query_block) * score_scale
        d_value_block = outer_rows(attn_probs.astype(jnp.bfloat16), grad_block)
        d_cum_rows = jnp.sum(d_scores, axis=1, dtype=jnp.float32)
        d_cum_cols = -jnp.sum(d_scores, axis=0, dtype=jnp.float32)
        return (d_query_block, d_key_block, d_value_block, d_cum_rows, d_cum_cols)

    dq_items, dk_items, dv_items, dcq_items, dck_items = lax.map(
        backward_item, (q_items, k_items, v_items, cq_items, ck_items, lse_items, da_items)
    )
    dc_own = dcq_items + dck_items[:, half_rows:]
    dc_left = dck_items[:, :half_rows]
    dc_left = dc_left.at[:, -1].add(jnp.sum(dc_own, axis=1))
    back_keys, back_values, back_cum = (
        shifted(to_slots(dk_items[:, :half_rows]).astype(jnp.bfloat16), "ctx", -1).astype(
            jnp.float32
        ),
        shifted(to_slots(dv_items[:, :half_rows]).astype(jnp.bfloat16), "ctx", -1).astype(
            jnp.float32
        ),
        shifted(to_slots_cum(dc_left).astype(jnp.bfloat16), "ctx", -1).astype(jnp.float32),
    )
    d_query = to_slots(dq_items).reshape(row_count, local_heads, head_size)
    d_key = (to_slots(dk_items[:, half_rows:]) + back_keys).reshape(
        row_count, local_heads, head_size
    )
    d_value = (to_slots(dv_items[:, half_rows:]) + back_values).reshape(row_count, head_cols)
    d_cum = to_slots_cum(dc_own) + back_cum
    d_log = jnp.flip(jnp.cumsum(jnp.flip(d_cum, 1), axis=1), 1)
    d_forget = d_log * jax.nn.sigmoid(-forget_pre)
    d_bias_own = jnp.sum(d_forget, axis=(0, 1))
    d_forget_low = d_forget.reshape(row_count, local_heads).astype(jnp.bfloat16)
    grad_forget = outer_rows(normed, d_forget_low)
    _, pull_query = jax.vjp(norm_rows, query_raw, qk_gain[0])
    d_query_raw, d_query_gain = pull_query(d_query)
    _, pull_key = jax.vjp(norm_rows, key_raw, qk_gain[1])
    d_key_raw, d_key_gain = pull_key(d_key)
    d_mixed = (
        jnp.stack(
            [
                d_query_raw.reshape(row_count, head_cols),
                d_key_raw.reshape(row_count, head_cols),
                d_value,
            ],
            axis=1,
        )
        .astype(jnp.bfloat16)
        .reshape(row_count, 3 * head_cols)
    )
    grad_qkv = outer_rows(normed, d_mixed).reshape(model_width, 3, head_cols)
    d_normed = (
        product_t(d_mixed, qkv_flat)
        + product_t(d_open, ogate_full)
        + product_t(d_forget_low, forget_full)
    )
    root = lax.rsqrt(jnp.mean(residual * residual, axis=1, keepdims=True) + epsilon)
    unit = residual * root
    d_unit = d_normed * gain_attn
    dot_part = (jnp.sum(d_unit * unit, axis=1) / model_width).reshape(slot_count, half_rows)
    d_unit_share, dot_full = (
        lax.psum_scatter(
            d_unit.reshape(slot_count, half_rows, model_width).astype(jnp.bfloat16),
            "tp",
            scatter_dimension=1,
            tiled=True,
        ).astype(jnp.float32),
        lax.psum_scatter(
            dot_part.astype(jnp.bfloat16), "tp", scatter_dimension=1, tiled=True
        ).astype(jnp.float32),
    )
    unit_share = own_slice(unit)
    root_share = own_slice(root)
    input_grad = (
        d_middle_share + root_share * (d_unit_share - unit_share * dot_full[:, :, None])
    ).astype(jnp.bfloat16)
    grad_parts = (
        lax.psum_scatter(
            grad_qkv.astype(jnp.bfloat16), ("shard", "ctx"), scatter_dimension=0, tiled=True
        ).astype(jnp.float32),
        lax.psum_scatter(
            grad_forget.astype(jnp.bfloat16), ("shard", "ctx"), scatter_dimension=0, tiled=True
        ).astype(jnp.float32),
        lax.psum_scatter(
            grad_ogate.astype(jnp.bfloat16), ("shard", "ctx"), scatter_dimension=0, tiled=True
        ).astype(jnp.float32),
        lax.psum_scatter(
            grad_out.astype(jnp.bfloat16), ("shard", "ctx"), scatter_dimension=0, tiled=True
        ).astype(jnp.float32),
        lax.psum_scatter(
            grad_gu.astype(jnp.bfloat16), ("shard", "ctx"), scatter_dimension=0, tiled=True
        ).astype(jnp.float32),
        lax.psum_scatter(
            grad_down.astype(jnp.bfloat16), ("shard", "ctx"), scatter_dimension=0, tiled=True
        ).astype(jnp.float32),
    )
    bias_full = lax.dynamic_update_slice_in_dim(
        jnp.zeros(forget_bias.shape, jnp.float32), d_bias_own, tensor_place * local_heads, 0
    )
    gain_attn_part = jnp.sum(d_normed * unit, axis=0)
    small_parts = lax.psum(
        (gain_attn_part, d_gain_mlp_own, jnp.stack([d_query_gain, d_key_gain]), bias_full),
        ("shard", "ctx", "tp"),
    )
    return (
        output,
        input_grad,
        grad_parts[0],
        grad_parts[1],
        small_parts[3],
        grad_parts[2],
        grad_parts[3],
        grad_parts[4],
        grad_parts[5],
        small_parts[0],
        small_parts[1],
        small_parts[2],
    )


def solution(mesh):
    return jax.shard_map(
        body,
        mesh=mesh,
        in_specs=(
            P("shard", ("ctx", "tp"), None),
            P("shard", ("ctx", "tp"), None),
            P("shard"),
            P(("shard", "ctx"), None, "tp"),
            P(("shard", "ctx"), "tp"),
            P(),
            P(("shard", "ctx"), "tp"),
            P(("shard", "ctx"), "tp"),
            P(("shard", "ctx"), None, "tp"),
            P(("shard", "ctx"), "tp"),
            P(),
            P(),
            P(),
        ),
        out_specs=(
            P("shard", ("ctx", "tp"), None),
            P("shard", ("ctx", "tp"), None),
            P(("shard", "ctx"), None, "tp"),
            P(("shard", "ctx"), "tp"),
            P(),
            P(("shard", "ctx"), "tp"),
            P(("shard", "ctx"), "tp"),
            P(("shard", "ctx"), None, "tp"),
            P(("shard", "ctx"), "tp"),
            P(),
            P(),
            P(),
        ),
        check_vma=False,
    )
```

profile of v0, /device:TPU:0, one launch (start us, length us, event | category | flops | bytes accessed | tf_op | source)
XLA Modules:
  0.0 1049.7 jit_solution(11627350117377922482)
XLA Ops:
  11.9 10.6 %all-gather = bf16[8,192,6]{1,2,0:T(8,128)(2,1)S(1)} all-gather(bf16[1,192,6]{1,2,0:T(8,128)(2,1)} %bitcast.510), channel_id=1, replica_groups=mesh['shard'=4,'ctx'=2,'tp'=4] {'shard','ctx'}, dimensions={0}, use_global_device_ids=true | all-gather | bytes 20736 | tf_op jit(solution)/shard_map/all_gather | solution.py:70
  24.6 24.8 %all-gather.9.cloned.1.call-done = bf16[1,512,1536]{2,1,0:T(8,128)(2,1)} async-done(((bf16[1,128,1536]{2,1,0:T(8,128)(2,1)}), bf16[1,512,1536]{2,1,0:T(8,128)(2,1)}) %all-gather.9.cloned.1.call-update) | async-done | bytes 1572880 | tf_op jit(solution)/shard_map/all_gather | solution.py:65
  59.5 24.7 %all-gather.11.cloned.1.call-done = bf16[1536,3,384]{2,0,1:T(8,128)(2,1)} async-done(((bf16[192,3,384]{2,0,1:T(8,128)(2,1)}), bf16[1536,3,384]{2,0,1:T(8,128)(2,1)}) %all-gather.11.cloned.1.call-update) | async-done | bytes 3538960 | tf_op jit(solution)/shard_map/all_gather | solution.py:69
  84.2 6.1 copy.92
  90.3 4.1 fusion.41
  96.7 2.9 collective-permute-start
  106.8 3.3 fusion.74
  118.7 37.0 %while.31 = (s32[]{:T(128)}, f32[6,512,64]{1,2,0:T(8,128)}, f32[6,512]{1,0:T(8,128)S(1)}, bf16[6,512,64]{2,1,0:T(8,128)(2,1)}, bf16[6,1024,64]{2,1,0:T(8,128)(2,...) while((s32[]{:T(128)}, f32[6,512,64]{1,2,0:T(8,128)}, ...), condition=%wide.region_8.9_spmd, body=%wide.region_5.8_spmd.sunk | while | flops 139460096 | bytes 7643265 | solution.py:151
  128.7 2.3 fusion.162
  134.9 2.2 fusion.162
  156.2 3.4 fusion.84
  159.7 4.0 fusion.126
  168.9 116.0 %all-reduce.5.cloned.1.call-done = f32[512,1536]{1,0:T(8,128)} async-done(((f32[512,1536]{1,0:T(8,128)}), f32[512,1536]{1,0:T(8,128)}) %all-reduce.5.cloned.1.call-update) | async-done | bytes 3145744 | tf_op jit(solution)/shard_map/psum | solution.py:158
  284.9 2.8 multiply_reduce_fusion.5
  289.3 42.5 %all-gather.17.cloned.1.call-done = bf16[1536,2,1024]{2,0,1:T(8,128)(2,1)} async-done(((bf16[192,2,1024]{2,0,1:T(8,128)(2,1)}), bf16[1536,2,1024]{2,0,1:T(8,128)(2,1)}) %all-gather.17.cloned.1.call-update) | async-done | bytes 6291472 | tf_op jit(solution)/shard_map/all_gather | solution.py:73
  331.8 8.7 copy.104
  340.5 8.1 fusion.36
  348.6 21.9 %all-gather.21.cloned.1.call-done = bf16[1,512,1536]{2,1,0:T(8,128)(2,1)} async-done(((bf16[1,128,1536]{2,1,0:T(8,128)(2,1)}), bf16[1,512,1536]{2,1,0:T(8,128)(2,1)}) %all-gather.21.cloned.1.call-update) | async-done | bytes 1572880 | tf_op jit(solution)/shard_map/all_gather | solution.py:66
  370.5 33.1 %all-gather.19.cloned.1.call-done = bf16[1536,1024]{1,0:T(8,128)(2,1)} async-done(((bf16[192,1024]{1,0:T(8,128)(2,1)}), bf16[1536,1024]{1,0:T(8,128)(2,1)}) %all-gather.19.cloned.1.call-update) | async-done | bytes 3145744 | tf_op jit(solution)/shard_map/all_gather | solution.py:74
  403.6 5.9 fusion.52
  410.9 8.0 convolution_bitcast_fusion.2
  423.5 6.7 fusion.47
  430.5 109.7 %all-reduce.7.cloned.1.call-done = f32[512,1536]{1,0:T(8,128)} async-done(((f32[512,1536]{1,0:T(8,128)}), f32[512,1536]{1,0:T(8,128)}) %all-reduce.7.cloned.1.call-update) | async-done | bytes 3145744 | tf_op jit(solution)/shard_map/psum | solution.py:186
  540.2 3.4 multiply_reduce_fusion.1
  543.7 3.0 fusion.46
  552.2 97.2 %while.32 = (s32[]{:T(128)}, f32[6,512,64]{1,2,0:T(8,128)}, f32[6,1024,64]{1,2,0:T(8,128)}, f32[6,1024,64]{1,2,0:T(8,128)}, f32[6,512]{1,0:T(8,128)}, /*index=5*...) while((s32[]{:T(128)}, f32[6,512,64]{1,2,0:T(8,128)}, ...), condition=%wide.region_18.19_spmd, body=%wide.region_14.18_spmd.sunk | while | flops 342981632 | bytes 20376776 | solution.py:216
  667.2 2.3 fusion.80
  672.4 2.7 rev.7
  676.4 4.1 reduce-window.16
  691.2 2.7 rev.8
  695.9 2.6 convolution_convert_fusion.6
  700.6 2.3 multiply_reduce_fusion.6
  707.6 2.3 convolution_bitcast_fusion.3
  711.4 3.4 multiply_reduce_fusion.2
  715.7 6.4 convolution_convert_fusion.2
  722.2 3.7 convolution_convert_fusion.5
  729.0 5.8 convolution_convert_fusion.1
  734.9 3.1 maximum_convert_fusion
  738.0 4.0 copy.114
  742.0 8.9 convolution_convert_fusion
  755.5 41.1 %all-reduce.1 = (f32[24]{0:T(128)}, f32[1536]{0:T(1024)}, f32[1536]{0:T(1024)}, f32[2,64]{1,0:T(2,128)}) all-reduce(f32[24]{0:T(128)S(1)} %dynamic_update_slice.28, f32[1536]{0:T(1024)S(1)} %get-tuple-element.207, f32[1536]{0:T(1024)S(1)} %fusion.108, ...), channel_id=1, replica_groups=mesh['shard'=4,'ctx'=2,'tp'=4] {'shard','ctx','tp'}, use_global_device_ids=true, to_apply=%region_30.31 | all-reduce | flops 3224 | bytes 25792 | tf_op jit(solution)/shard_map/psum | solution.py:308
  797.5 8.2 reduce-scatter.26.cloned.1.call-done
  807.7 37.9 %reduce-scatter.20.cloned.1.call-done = bf16[192,384]{1,0:T(8,128)(2,1)} async-done(((bf16[1536,384]{1,0:T(8,128)(2,1)}), bf16[192,384]{1,0:T(8,128)(2,1)}) %reduce-scatter.20.cloned.1.call-update) | async-done | bytes 147472 | tf_op jit(solution)/shard_map/reduce_scatter | solution.py:291
  847.2 38.6 %reduce-scatter.22.cloned.1.call-done = bf16[192,384]{1,0:T(8,128)(2,1)} async-done(((bf16[1536,384]{1,0:T(8,128)(2,1)}), bf16[192,384]{1,0:T(8,128)(2,1)}) %reduce-scatter.22.cloned.1.call-update) | async-done | bytes 147472 | tf_op jit(solution)/shard_map/reduce_scatter | solution.py:294
  887.5 36.4 %reduce-scatter.16.cloned.1.call-done = bf16[1,128,1536]{2,1,0:T(8,128)(2,1)} async-done(((bf16[1,512,1536]{2,1,0:T(8,128)(2,1)}), bf16[1,128,1536]{2,1,0:T(8,128)(2,1)}) %reduce-scatter.16.cloned.1.call-update) | async-done | bytes 393232 | tf_op jit(solution)/shard_map/reduce_scatter | solution.py:269
  926.1 48.2 %reduce-scatter.18.cloned.1.call-done = bf16[192,3,384]{2,0,1:T(8,128)(2,1)} async-done(((bf16[1536,3,384]{2,0,1:T(8,128)(2,1)}), bf16[192,3,384]{2,0,1:T(8,128)(2,1)}) %reduce-scatter.18.cloned.1.call-update) | async-done | bytes 442384 | tf_op jit(solution)/shard_map/reduce_scatter | solution.py:285
  976.3 63.0 %reduce-scatter.24.cloned.1.call-done = bf16[192,2,1024]{2,0,1:T(8,128)(2,1)} async-done(((bf16[1536,2,1024]{2,0,1:T(8,128)(2,1)}), bf16[192,2,1024]{2,0,1:T(8,128)(2,1)}) %reduce-scatter.24.cloned.1.call-update) | async-done | bytes 786448 | tf_op jit(solution)/shard_map/reduce_scatter | solution.py:297
  1039.3 3.1 copy.116
  (419 shorter events, 243.9 us)
Async XLA Ops:
  7.2 17.4 %copy-start.69 = (f32[24]{0:T(128)S(1)}, f32[24]{0:T(128)}, u32[]{:S(2)}) copy-start(f32[24]{0:T(128)} %param.24) | copy-start | bytes 292
  7.2 42.2 %all-gather.9.cloned.1.call-start = ((), (), s32[]{:S(2)}) async-start(), calls=%async_computation.9 | async-start | bytes 1966080 | tf_op jit(solution)/shard_map/all_gather | solution.py:65
  7.9 76.3 %all-gather.11.cloned.1.call-start = ((), (), s32[]{:S(2)}) async-start(), calls=%async_computation.10 | async-start | bytes 3981312 | tf_op jit(solution)/shard_map/all_gather | solution.py:69
  8.7 42.5 %copy-start.59 = (f32[1536]{0:T(1024)S(1)}, f32[1536]{0:T(1024)}, u32[]{:S(2)}) copy-start(f32[1536]{0:T(1024)} %param.29) | copy-start | bytes 18436
  8.7 147.0 %all-gather.13.cloned.1.call-start = ((), (), s32[]{:S(2)}) async-start(), calls=%async_computation.11 | async-start | bytes 1327104 | tf_op jit(solution)/shard_map/all_gather | solution.py:71
  9.4 150.3 %all-gather.15.cloned.1.call-start = ((), (), s32[]{:S(2)}) async-start(), calls=%async_computation.12 | async-start | bytes 1327104 | tf_op jit(solution)/shard_map/all_gather | solution.py:72
  10.0 274.9 %all-reduce.5.cloned.1.call-start = ((), (), s32[]{:S(2)}) async-start(), calls=%async_computation.13 | async-start | bytes 6291456 | tf_op jit(solution)/shard_map/psum | solution.py:158
  11.5 84.3 %copy-start.49 = (f32[384]{0:T(512)}, f32[384]{0:T(512)S(1)}, u32[]{:S(2)}) copy-start(f32[384]{0:T(512)S(1)} %mul.513) | copy-start | bytes 4612
  22.7 30.5 %copy-start.39 = (bf16[1536,6]{0,1:T(8,128)(2,1)}, bf16[1536,6]{0,1:T(8,128)(2,1)S(1)}, u32[]{:S(2)}) copy-start(bf16[1536,6]{0,1:T(8,128)(2,1)S(1)} %reshape.771) | copy-start | bytes 55300
  51.2 39.1 %copy-start.57 = (f32[512]{0:T(512)}, f32[512]{0:T(512)S(1)}, u32[]{:S(2)}) copy-start(f32[512]{0:T(512)S(1)} %add_rsqrt_fusion) | copy-start | bytes 6148
  53.2 5.0 copy-start.42
  55.5 2.4 collective-permute-start.1
  59.5 30.8 %copy-start.2 = (bf16[1,512,1536]{2,1,0:T(8,128)(2,1)S(1)}, bf16[1,512,1536]{2,1,0:T(8,128)(2,1)}, u32[]{:S(2)}) copy-start(bf16[1,512,1536]{2,1,0:T(8,128)(2,1)} %all-gather.9.cloned.1.call-done) | copy-start | bytes 4718596
  94.4 7.8 copy-start.4
  94.6 7.8 copy-start.9
  94.6 9.4 copy-start.6
  95.7 6.0 copy-start.37
  95.8 5.9 copy-start.35
  96.7 13.4 %collective-permute-start = (bf16[1,512,384]{1,2,0:T(8,128)(2,1)}, bf16[1,512,384]{1,2,0:T(8,128)(2,1)}, u32[]{:S(2)}, u32[]{:S(2)}) collective-permute-start(bf16[1,512,384]{1,2,0:T(8,128)(2,1)} %multiply_convert_fusion.9), channel_id=1, source_target_pairs={{0,4},{1,5},{2,6},{3,7},{8,12},{9,13},{10,14},{11,15},{16,20},{17,... | collective-permute-start | bytes 1179656 | tf_op jit(solution)/shard_map/ppermute | solution.py:13
  99.6 12.7 %collective-permute-start.2 = (bf16[1,512,384]{1,2,0:T(8,128)(2,1)}, bf16[1,512,384]{1,2,0:T(8,128)(2,1)}, u32[]{:S(2)}, u32[]{:S(2)}) collective-permute-start(bf16[1,512,384]{1,2,0:T(8,128)(2,1)} %slice_bitcast_fusion.5), channel_id=1, source_target_pairs={{0,4},{1,5},{2,6},{3,7},{8,12},{9,13},{10,14},{11,15},{16,20},{17,... | collective-permute-start | bytes 1179656 | tf_op jit(solution)/shard_map/ppermute | solution.py:13
  155.6 4.0 copy-start.10
  163.7 168.1 %all-gather.17.cloned.1.call-start = ((), (), s32[]{:S(2)}) async-start(), calls=%async_computation.14 | async-start | bytes 7077888 | tf_op jit(solution)/shard_map/all_gather | solution.py:73
  165.9 204.6 %all-gather.21.cloned.1.call-start = ((), (), s32[]{:S(2)}) async-start(), calls=%async_computation.17 | async-start | bytes 1966080 | tf_op jit(solution)/shard_map/all_gather | solution.py:66
  166.7 236.9 %all-gather.19.cloned.1.call-start = ((), (), s32[]{:S(2)}) async-start(), calls=%async_computation.15 | async-start | bytes 3538944 | tf_op jit(solution)/shard_map/all_gather | solution.py:74
  167.4 372.7 %all-reduce.7.cloned.1.call-start = ((), (), s32[]{:S(2)}) async-start(), calls=%async_computation.18 | async-start | bytes 6291456 | tf_op jit(solution)/shard_map/psum | solution.py:186
  287.8 252.4 %copy-start = (f32[512,1536]{1,0:T(8,128)}, f32[512,1536]{1,0:T(8,128)S(1)}, u32[]{:S(2)}) copy-start(f32[512,1536]{1,0:T(8,128)S(1)} %get-tuple-element.267) | copy-start | bytes 9437188
  418.9 332.6 %reduce-scatter.14.cloned.1.call-start = ((), (), s32[]{:S(2)}) async-start(), calls=%async_computation.16 | async-start | bytes 1966080 | tf_op jit(solution)/shard_map/reduce_scatter | solution.py:167
  430.2 323.7 %reduce-scatter.30.cloned.1.call-start = ((), (), s32[]{:S(2)}) async-start(), calls=%async_computation.26 | async-start | bytes 442368
  653.4 51.8 %collective-permute-start.4 = (bf16[1,512,384]{1,2,0:T(8,128)(2,1)}, bf16[1,512,384]{1,2,0:T(8,128)(2,1)}, u32[]{:S(2)}, u32[]{:S(2)}) collective-permute-start(bf16[1,512,384]{1,2,0:T(8,128)(2,1)} %bitcast.100), channel_id=1, source_target_pairs={{4,0},{5,1},{6,2},{7,3},{12,8},{13,9},{14,10},{15,11},{20,16},{21,... | collective-permute-start | bytes 1179656 | tf_op jit(solution)/shard_map/ppermute | solution.py:13
  656.6 44.0 %collective-permute-start.3 = (bf16[1,512,384]{1,2,0:T(8,128)(2,1)}, bf16[1,512,384]{1,2,0:T(8,128)(2,1)}, u32[]{:S(2)}, u32[]{:S(2)}) collective-permute-start(bf16[1,512,384]{1,2,0:T(8,128)(2,1)} %bitcast.90), channel_id=1, source_target_pairs={{4,0},{5,1},{6,2},{7,3},{12,8},{13,9},{14,10},{15,11},{20,16},{21,... | collective-permute-start | bytes 1179656 | tf_op jit(solution)/shard_map/ppermute | solution.py:13
  665.8 5.1 copy-start.24
  665.8 6.0 copy-start.34
  665.8 6.0 copy-start.38
  665.8 6.0 collective-permute-start.5
  700.3 96.4 %reduce-scatter.28.cloned.1.call-start = ((), (), s32[]{:S(2)}) async-start(), calls=%async_computation.25 | async-start | bytes 163840
  705.2 4.7 copy-start.27
  705.2 4.7 copy-start.29
  711.4 4.3 copy-start.66
  715.7 90.0 %reduce-scatter.26.cloned.1.call-start = ((), (), s32[]{:S(2)}) async-start(), calls=%async_computation.24 | async-start | bytes 3538944 | tf_op jit(solution)/shard_map/reduce_scatter | solution.py:300
  722.2 123.4 %reduce-scatter.20.cloned.1.call-start = ((), (), s32[]{:S(2)}) async-start(), calls=%async_computation.21 | async-start | bytes 1327104 | tf_op jit(solution)/shard_map/reduce_scatter | solution.py:291
  725.9 159.9 %reduce-scatter.22.cloned.1.call-start = ((), (), s32[]{:S(2)}) async-start(), calls=%async_computation.22 | async-start | bytes 1327104 | tf_op jit(solution)/shard_map/reduce_scatter | solution.py:294
  728.0 195.8 %reduce-scatter.16.cloned.1.call-start = ((), (), s32[]{:S(2)}) async-start(), calls=%async_computation.19 | async-start | bytes 1966080 | tf_op jit(solution)/shard_map/reduce_scatter | solution.py:269
  728.6 245.7 %reduce-scatter.18.cloned.1.call-start = ((), (), s32[]{:S(2)}) async-start(), calls=%async_computation.20 | async-start | bytes 3981312 | tf_op jit(solution)/shard_map/reduce_scatter | solution.py:285
  734.9 304.4 %reduce-scatter.24.cloned.1.call-start = ((), (), s32[]{:S(2)}) async-start(), calls=%async_computation.23 | async-start | bytes 7077888 | tf_op jit(solution)/shard_map/reduce_scatter | solution.py:297
  738.0 4.0 copy-start.45
  738.0 4.0 copy-start.52
  750.8 4.6 copy-start.56
  750.9 4.7 copy-start.67
  (51 other events, 109.9 us)
Sparse Core Ops, SparseCore 0:
  9.6 39.7 all-gather.8
  51.3 32.8 all-gather.10
  86.1 24.0 all-gather.12
  112.0 24.0 all-gather.14
  163.8 121.0 all-reduce.4
  287.2 44.5 all-gather.16
  333.4 37.0 all-gather.20
  372.4 31.1 all-gather.18
  419.0 121.0 all-reduce.6
  542.3 34.2 reduce-scatter.13
  700.4 35.1 reduce-scatter.29
  738.2 19.1 reduce-scatter.27
  761.2 44.4 reduce-scatter.25
  808.8 36.7 reduce-scatter.19
  849.0 36.7 reduce-scatter.21
  888.6 35.2 reduce-scatter.15
  927.2 47.0 reduce-scatter.17
  977.5 61.7 reduce-scatter.23
where the time goes:
time: 1060 us; the launch traced here: 1050 us
  waiting for transfers between devices  611 us (58%)
  matrix products  162 us (15%)
  local copies, waits for them, and re-layouts  121 us (11%)
  other arithmetic  75.4 us (7%)
  blocking collectives  51.8 us (5%)
  between operations  16.4 us (2%)
  starting transfers between devices  12.2 us (1%)
    psum x1, waiting for transfers between devices, body(): branch_full = lax.psum(branch_part, 'tp')  116 us
    psum x1, waiting for transfers between devices, body(): d_normed_mid = lax.psum(d_mid_terms, 'tp')  110 us
    reduce_scatter x1, waiting for transfers between devices, body(): lax.psum_scatter(grad_gu.astype(jnp.bfloat16), ('shard', 'ctx'), scatter_...  63 us
    dot_general x24, matrix products, product_t(): lax.dot_general(left, right, (((1,), (1,)), ((), ())), preferred_element_...  58 us
    dot_general x18, matrix products, outer_rows(): lax.dot_general(left, right, (((0,), (0,)), ((), ())), preferred_element_...  52.8 us
    dot_general x18, matrix products, product(): return jnp.dot(left, right, preferred_element_type=jnp.float32)  51.2 us
    reduce_scatter x1, waiting for transfers between devices, body(): lax.psum_scatter(grad_qkv.astype(jnp.bfloat16), ('shard', 'ctx'), scatter...  48.2 us
    all_gather x1, waiting for transfers between devices, body(): lax.all_gather(w_gu, ('shard', 'ctx'), axis=0, tiled=True)  42.5 us
  transfers between devices with their start and end apart: 24, of which 14 were waited for; matrix products, arithmetic and copies ran while one was open for 31% of the time, Pallas kernels for 0%

commit v1 on v0

--- a/solution.py
+++ b/solution.py
@@ -1,3 +1,4 @@
+import functools
 import math
 import jax
 import jax.numpy as jnp
@@ -5,6 +6,44 @@
 from jax.sharding import PartitionSpec as P
 
 epsilon = 1e-06
+
+
+def make_things(local_array, device_axis):
+    f_next, spare, left_arr = (
+        lax.axis_size(device_axis),
+        lax.axis_index(device_axis),
+        local_array.shape[1],
+    )
+    front = lax.dynamic_update_slice_in_dim(
+        jnp.zeros(
+            [u * f_next if tick == 1 else u for tick, u in enumerate(local_array.shape)],
+            local_array.dtype,
+        ),
+        local_array,
+        spare * left_arr,
+        axis=1,
+    )
+    v_next = r1 = local_array
+    for to_i in range(1, f_next // 2 + 1):
+        v_next = lax.ppermute(
+            v_next, device_axis, list(map(lambda tick: (tick, (tick + 1) % f_next), range(f_next)))
+        )
+        front = lax.dynamic_update_slice_in_dim(
+            front, v_next, (spare - to_i) % f_next * left_arr, axis=1
+        )
+        if 2 * to_i < f_next:
+            r1 = lax.ppermute(
+                r1,
+                device_axis,
+                perm=list(map(lambda tick: (tick, (tick - 1) % f_next), range(f_next))),
+            )
+            front = lax.dynamic_update_slice_in_dim(
+                front, r1, (spare + to_i) % f_next * left_arr, axis=1
+            )
+    return front
+
+
+leaf_choose = functools.partial(make_things, device_axis="tp")
 
 
 def shifted(block, axis, distance):
@@ -62,7 +101,7 @@
     score_scale = 1.0 / math.sqrt(head_size)
     own_start = tensor_place * own_rows
     full_tokens, full_cot = (
-        lax.all_gather(tokens, "tp", axis=1, tiled=True),
+        leaf_choose(tokens),
         lax.all_gather(cotangent, "tp", axis=1, tiled=True),
     )
     qkv_full, forget_full, ogate_full, out_full, gu_full, down_full = (

time: 1060 us -> 1030 us (0.972)
  waiting for transfers between devices: 611 us -> 572 us
    all_gather x1 -> x0, waiting for transfers between devices: 24.8 us -> none  [body(): lax.all_gather(tokens, 'tp', axis=1, tiled=True)]
    all_gather x1, waiting for transfers between devices: 24.7 us -> 0.01 us  [body(): lax.all_gather(w_qkv, ('shard', 'ctx'), axis=0, tiled=True)]
    ppermute x0 -> x3, waiting for transfers between devices: none -> 13.1 us  [the longest x2 9.63 us: make_things(): lax.ppermute(v_next, device_axis, list(map(lambda tick: (tick, (tick + 1)...]
  transfers between devices with their start and end apart: 24 -> 26, of which waited for: 14 -> 14; matrix products, arithmetic and copies ran while one was open for 31% -> 32% of each run, Pallas kernels for 0% -> 0%
where the time goes in v1:
time: 1030 us; the launch traced here: 1010 us
  waiting for transfers between devices  572 us (56%)
  matrix products  161 us (16%)
  local copies, waits for them, and re-layouts  121 us (12%)
  other arithmetic  74 us (7%)
  blocking collectives  50.5 us (5%)
  starting transfers between devices  17.2 us (2%)
  between operations  15.8 us (2%)
    psum x1, waiting for transfers between devices, body(): branch_full = lax.psum(branch_part, 'tp')  115 us
    psum x1, waiting for transfers between devices, body(): d_normed_mid = lax.psum(d_mid_terms, 'tp')  110 us
    reduce_scatter x1, waiting for transfers between devices, body(): lax.psum_scatter(grad_gu.astype(jnp.bfloat16), ('shard', 'ctx'), scatter_...  63 us
    dot_general x24, matrix products, product_t(): lax.dot_general(left, right, (((1,), (1,)), ((), ())), preferred_element_...  58 us
    dot_general x18, matrix products, outer_rows(): lax.dot_general(left, right, (((0,), (0,)), ((), ())), preferred_element_...  52.9 us
    dot_general x18, matrix products, product(): return jnp.dot(left, right, preferred_element_type=jnp.float32)  49.8 us
    reduce_scatter x1, waiting for transfers between devices, body(): lax.psum_scatter(grad_qkv.astype(jnp.bfloat16), ('shard', 'ctx'), scatter...  48.2 us
    all_gather x1, waiting for transfers between devices, body(): lax.all_gather(w_gu, ('shard', 'ctx'), axis=0, tiled=True)  42.5 us
  transfers between devices with their start and end apart: 26, of which 14 were waited for; matrix products, arithmetic and copies ran while one was open for 32% of the time, Pallas kernels for 0%

profile of v1, /device:TPU:0, one launch (start us, length us, event | category | flops | bytes accessed | tf_op | source)
XLA Modules:
  0.0 1011.7 jit_solution(4696590939573946795)
XLA Ops:
  8.7 3.1 collective-permute-start
  15.9 9.4 all-gather
  27.6 3.4 collective-permute-done.1
  31.0 9.6 collective-permute-done.2
  47.7 6.0 copy.92
  53.7 4.2 fusion.38
  60.2 3.0 collective-permute-start.3
  70.4 3.3 fusion.68
  82.2 36.9 %while.31 = (s32[]{:T(128)}, f32[6,512,64]{1,2,0:T(8,128)}, f32[6,512]{1,0:T(8,128)S(1)}, bf16[6,512,64]{2,1,0:T(8,128)(2,1)}, bf16[6,1024,64]{2,1,0:T(8,128)(2,...) while((s32[]{:T(128)}, f32[6,512,64]{1,2,0:T(8,128)}, ...), condition=%wide.region_8.9_spmd, body=%wide.region_5.8_spmd.sunk | while | flops 139460096 | bytes 7643265 | solution.py:190
  92.2 2.2 fusion.152
  119.8 3.5 fusion.78
  123.2 4.0 fusion.116
  132.1 115.3 %all-reduce.5.cloned.1.call-done = f32[512,1536]{1,0:T(8,128)} async-done(((f32[512,1536]{1,0:T(8,128)}), f32[512,1536]{1,0:T(8,128)}) %all-reduce.5.cloned.1.call-update) | async-done | bytes 3145744 | tf_op jit(solution)/shard_map/psum | solution.py:197
  247.3 2.8 multiply_reduce_fusion.5
  251.7 42.5 %all-gather.14.cloned.1.call-done = bf16[1536,2,1024]{2,0,1:T(8,128)(2,1)} async-done(((bf16[192,2,1024]{2,0,1:T(8,128)(2,1)}), bf16[1536,2,1024]{2,0,1:T(8,128)(2,1)}) %all-gather.14.cloned.1.call-update) | async-done | bytes 6291472 | tf_op jit(solution)/shard_map/all_gather | solution.py:112
  294.2 8.7 copy.104
  302.9 8.0 fusion.36
  310.9 21.8 %all-gather.18.cloned.1.call-done = bf16[1,512,1536]{2,1,0:T(8,128)(2,1)} async-done(((bf16[1,128,1536]{2,1,0:T(8,128)(2,1)}), bf16[1,512,1536]{2,1,0:T(8,128)(2,1)}) %all-gather.18.cloned.1.call-update) | async-done | bytes 1572880 | tf_op jit(solution)/shard_map/all_gather | solution.py:105
  332.8 33.1 %all-gather.16.cloned.1.call-done = bf16[1536,1024]{1,0:T(8,128)(2,1)} async-done(((bf16[192,1024]{1,0:T(8,128)(2,1)}), bf16[1536,1024]{1,0:T(8,128)(2,1)}) %all-gather.16.cloned.1.call-update) | async-done | bytes 3145744 | tf_op jit(solution)/shard_map/all_gather | solution.py:113
  365.8 5.9 fusion.47
  373.1 8.0 convolution_bitcast_fusion.2
  385.8 6.7 fusion.42
  392.8 109.6 %all-reduce.7.cloned.1.call-done = f32[512,1536]{1,0:T(8,128)} async-done(((f32[512,1536]{1,0:T(8,128)}), f32[512,1536]{1,0:T(8,128)}) %all-reduce.7.cloned.1.call-update) | async-done | bytes 3145744 | tf_op jit(solution)/shard_map/psum | solution.py:225
  502.5 3.4 multiply_reduce_fusion.1
  506.0 3.0 fusion.41
  514.5 97.3 %while.32 = (s32[]{:T(128)}, f32[6,512,64]{1,2,0:T(8,128)}, f32[6,1024,64]{1,2,0:T(8,128)}, f32[6,1024,64]{1,2,0:T(8,128)}, f32[6,512]{1,0:T(8,128)}, /*index=5*...) while((s32[]{:T(128)}, f32[6,512,64]{1,2,0:T(8,128)}, ...), condition=%wide.region_18.19_spmd, body=%wide.region_14.18_spmd.sunk | while | flops 342981632 | bytes 20376776 | solution.py:255
  629.6 2.4 fusion.74
  634.9 2.7 rev.7
  638.9 4.1 reduce-window.16
  653.7 2.7 rev.8
  658.3 2.6 convolution_convert_fusion.6
  663.2 2.3 multiply_reduce_fusion.6
  670.2 2.3 convolution_bitcast_fusion.3
  673.9 3.4 multiply_reduce_fusion.2
  678.3 6.4 convolution_convert_fusion.2
  684.7 3.7 convolution_convert_fusion.5
  691.6 5.8 convolution_convert_fusion.1
  697.5 3.1 maximum_convert_fusion
  700.6 4.0 copy.114
  704.5 8.8 convolution_convert_fusion
  718.1 41.2 %all-reduce.1 = (f32[24]{0:T(128)}, f32[1536]{0:T(1024)}, f32[1536]{0:T(1024)}, f32[2,64]{1,0:T(2,128)}) all-reduce(f32[24]{0:T(128)S(1)} %dynamic_update_slice.48, f32[1536]{0:T(1024)S(1)} %get-tuple-element.207, f32[1536]{0:T(1024)S(1)} %fusion.102, ...), channel_id=1, replica_groups=mesh['shard'=4,'ctx'=2,'tp'=4] {'shard','ctx','tp'}, use_global_device_ids=true, to_apply=%region_30.31 | all-reduce | flops 3224 | bytes 25792 | tf_op jit(solution)/shard_map/psum | solution.py:347
  760.0 8.2 reduce-scatter.26.cloned.1.call-done
  770.2 38.1 %reduce-scatter.20.cloned.1.call-done = bf16[192,384]{1,0:T(8,128)(2,1)} async-done(((bf16[1536,384]{1,0:T(8,128)(2,1)}), bf16[192,384]{1,0:T(8,128)(2,1)}) %reduce-scatter.20.cloned.1.call-update) | async-done | bytes 147472 | tf_op jit(solution)/shard_map/reduce_scatter | solution.py:330
  809.9 38.6 %reduce-scatter.22.cloned.1.call-done = bf16[192,384]{1,0:T(8,128)(2,1)} async-done(((bf16[1536,384]{1,0:T(8,128)(2,1)}), bf16[192,384]{1,0:T(8,128)(2,1)}) %reduce-scatter.22.cloned.1.call-update) | async-done | bytes 147472 | tf_op jit(solution)/shard_map/reduce_scatter | solution.py:333
  850.1 36.4 %reduce-scatter.16.cloned.1.call-done = bf16[1,128,1536]{2,1,0:T(8,128)(2,1)} async-done(((bf16[1,512,1536]{2,1,0:T(8,128)(2,1)}), bf16[1,128,1536]{2,1,0:T(8,128)(2,1)}) %reduce-scatter.16.cloned.1.call-update) | async-done | bytes 393232 | tf_op jit(solution)/shard_map/reduce_scatter | solution.py:308
  888.7 48.2 %reduce-scatter.18.cloned.1.call-done = bf16[192,3,384]{2,0,1:T(8,128)(2,1)} async-done(((bf16[1536,3,384]{2,0,1:T(8,128)(2,1)}), bf16[192,3,384]{2,0,1:T(8,128)(2,1)}) %reduce-scatter.18.cloned.1.call-update) | async-done | bytes 442384 | tf_op jit(solution)/shard_map/reduce_scatter | solution.py:324
  938.9 63.0 %reduce-scatter.24.cloned.1.call-done = bf16[192,2,1024]{2,0,1:T(8,128)(2,1)} async-done(((bf16[1536,2,1024]{2,0,1:T(8,128)(2,1)}), bf16[192,2,1024]{2,0,1:T(8,128)(2,1)}) %reduce-scatter.24.cloned.1.call-update) | async-done | bytes 786448 | tf_op jit(solution)/shard_map/reduce_scatter | solution.py:336
  1001.9 3.1 copy.116
  (429 shorter events, 244.1 us)
Async XLA Ops:
  7.2 20.1 %copy-start.70 = (f32[24]{0:T(128)S(1)}, f32[24]{0:T(128)}, u32[]{:S(2)}) copy-start(f32[24]{0:T(128)} %param.24) | copy-start | bytes 292
  7.2 40.5 %all-gather.8.cloned.1.call-start = ((), (), s32[]{:S(2)}) async-start(), calls=%async_computation.9 | async-start | bytes 3981312 | tf_op jit(solution)/shard_map/all_gather | solution.py:108
  7.9 19.5 %copy-start.30 = (bf16[1,128,1536]{2,1,0:T(8,128)(2,1)S(1)}, bf16[1,128,1536]{2,1,0:T(8,128)(2,1)}, u32[]{:S(2)}) copy-start(bf16[1,128,1536]{2,1,0:T(8,128)(2,1)} %param.19) | copy-start | bytes 1179652
  7.9 111.3 %all-gather.10.cloned.1.call-start = ((), (), s32[]{:S(2)}) async-start(), calls=%async_computation.10 | async-start | bytes 1327104 | tf_op jit(solution)/shard_map/all_gather | solution.py:110
  8.7 114.5 %all-gather.12.cloned.1.call-start = ((), (), s32[]{:S(2)}) async-start(), calls=%async_computation.11 | async-start | bytes 1327104 | tf_op jit(solution)/shard_map/all_gather | solution.py:111
  8.7 18.8 %collective-permute-start = (bf16[1,128,1536]{2,1,0:T(8,128)(2,1)}, bf16[1,128,1536]{2,1,0:T(8,128)(2,1)S(1)}, u32[]{:S(2)}, u32[]{:S(2)}) collective-permute-start(bf16[1,128,1536]{2,1,0:T(8,128)(2,1)} %param.19), channel_id=1, source_target_pairs={{0,1},{1,2},{2,3},{3,0},{4,5},{5,6},{6,7},{7,4},{8,9},{9,10},{10,1... | collective-permute-start | bytes 1179656 | tf_op jit(solution)/shard_map/ppermute | solution.py:28
  11.8 19.2 %collective-permute-start.1 = (bf16[1,128,1536]{2,1,0:T(8,128)(2,1)}, bf16[1,128,1536]{2,1,0:T(8,128)(2,1)S(1)}, u32[]{:S(2)}, u32[]{:S(2)}) collective-permute-start(bf16[1,128,1536]{2,1,0:T(8,128)(2,1)} %param.19), channel_id=1, source_target_pairs={{0,3},{1,0},{2,1},{3,2},{4,7},{5,4},{6,5},{7,6},{8,11},{9,8},{10,9... | collective-permute-start | bytes 1179656 | tf_op jit(solution)/shard_map/ppermute | solution.py:35
  13.9 233.4 %all-reduce.5.cloned.1.call-start = ((), (), s32[]{:S(2)}) async-start(), calls=%async_computation.12 | async-start | bytes 6291456 | tf_op jit(solution)/shard_map/psum | solution.py:197
  15.9 43.4 %copy-start.50 = (f32[384]{0:T(512)}, f32[384]{0:T(512)S(1)}, u32[]{:S(2)}) copy-start(f32[384]{0:T(512)S(1)} %mul.512) | copy-start | bytes 4612
  25.4 15.8 %copy-start.40 = (bf16[1536,6]{0,1:T(8,128)(2,1)}, bf16[1536,6]{0,1:T(8,128)(2,1)S(1)}, u32[]{:S(2)}) copy-start(bf16[1536,6]{0,1:T(8,128)(2,1)S(1)} %reshape.750) | copy-start | bytes 55300
  27.5 13.7 %copy-start.60 = (f32[1536]{0:T(1024)S(1)}, f32[1536]{0:T(1024)}, u32[]{:S(2)}) copy-start(f32[1536]{0:T(1024)} %param.29) | copy-start | bytes 18436
  27.5 13.2 %collective-permute-start.2 = (bf16[1,128,1536]{2,1,0:T(8,128)(2,1)S(1)}, bf16[1,128,1536]{2,1,0:T(8,128)(2,1)S(1)}, u32[]{:S(2)}, u32[]{:S(2)}) collective-permute-start(bf16[1,128,1536]{2,1,0:T(8,128)(2,1)S(1)} %collective-permute-done), channel_id=1, source_target_pairs={{0,1},{1,2},{2,3},{3,0},{4,5},{5,6},{6,7},{7,4},{8,9},{9,10},{10,1... | collective-permute-start | bytes 1179656 | tf_op jit(solution)/shard_map/ppermute | solution.py:28
  40.7 79.0 %copy-start.1 = (bf16[512,1536]{1,0:T(8,128)(2,1)}, bf16[512,1536]{1,0:T(8,128)(2,1)S(1)}, u32[]{:S(2)}) copy-start(bf16[512,1536]{1,0:T(8,128)(2,1)S(1)} %bitcast_dynamic-update-slice_fusion) | copy-start | bytes 4718596
  41.1 12.6 %copy-start.58 = (f32[512]{0:T(512)}, f32[512]{0:T(512)S(1)}, u32[]{:S(2)}) copy-start(f32[512]{0:T(512)S(1)} %add_rsqrt_fusion) | copy-start | bytes 6148
  41.7 12.0 %copy-start.43 = (f32[512,6]{0,1:T(8,128)}, f32[512,6]{0,1:T(8,128)S(1)}, u32[]{:S(2)}) copy-start(f32[512,6]{0,1:T(8,128)S(1)} %convolution_add_fusion.2) | copy-start | bytes 36868
  44.0 2.1 collective-permute-start.4
  57.9 7.9 copy-start.4
  58.0 7.9 copy-start.9
  58.0 9.5 copy-start.6
  59.1 6.1 copy-start.38
  59.2 6.0 copy-start.36
  60.2 13.5 %collective-permute-start.3 = (bf16[1,512,384]{1,2,0:T(8,128)(2,1)}, bf16[1,512,384]{1,2,0:T(8,128)(2,1)}, u32[]{:S(2)}, u32[]{:S(2)}) collective-permute-start(bf16[1,512,384]{1,2,0:T(8,128)(2,1)} %multiply_convert_fusion.9), channel_id=1, source_target_pairs={{0,4},{1,5},{2,6},{3,7},{8,12},{9,13},{10,14},{11,15},{16,20},{17,... | collective-permute-start | bytes 1179656 | tf_op jit(solution)/shard_map/ppermute | solution.py:52
  63.1 12.6 %collective-permute-start.5 = (bf16[1,512,384]{1,2,0:T(8,128)(2,1)}, bf16[1,512,384]{1,2,0:T(8,128)(2,1)}, u32[]{:S(2)}, u32[]{:S(2)}) collective-permute-start(bf16[1,512,384]{1,2,0:T(8,128)(2,1)} %slice_bitcast_fusion.5), channel_id=1, source_target_pairs={{0,4},{1,5},{2,6},{3,7},{8,12},{9,13},{10,14},{11,15},{16,20},{17,... | collective-permute-start | bytes 1179656 | tf_op jit(solution)/shard_map/ppermute | solution.py:52
  127.2 167.0 %all-gather.14.cloned.1.call-start = ((), (), s32[]{:S(2)}) async-start(), calls=%async_computation.13 | async-start | bytes 7077888 | tf_op jit(solution)/shard_map/all_gather | solution.py:112
  129.5 203.3 %all-gather.18.cloned.1.call-start = ((), (), s32[]{:S(2)}) async-start(), calls=%async_computation.16 | async-start | bytes 1966080 | tf_op jit(solution)/shard_map/all_gather | solution.py:105
  130.0 235.8 %all-gather.16.cloned.1.call-start = ((), (), s32[]{:S(2)}) async-start(), calls=%async_computation.14 | async-start | bytes 3538944 | tf_op jit(solution)/shard_map/all_gather | solution.py:113
  130.8 371.6 %all-reduce.7.cloned.1.call-start = ((), (), s32[]{:S(2)}) async-start(), calls=%async_computation.17 | async-start | bytes 6291456 | tf_op jit(solution)/shard_map/psum | solution.py:225
  250.2 252.2 %copy-start = (f32[512,1536]{1,0:T(8,128)}, f32[512,1536]{1,0:T(8,128)S(1)}, u32[]{:S(2)}) copy-start(f32[512,1536]{1,0:T(8,128)S(1)} %get-tuple-element.267) | copy-start | bytes 9437188
  381.2 332.9 %reduce-scatter.14.cloned.1.call-start = ((), (), s32[]{:S(2)}) async-start(), calls=%async_computation.15 | async-start | bytes 1966080 | tf_op jit(solution)/shard_map/reduce_scatter | solution.py:206
  392.5 323.9 %reduce-scatter.30.cloned.1.call-start = ((), (), s32[]{:S(2)}) async-start(), calls=%async_computation.25 | async-start | bytes 442368
  615.8 52.0 %collective-permute-start.7 = (bf16[1,512,384]{1,2,0:T(8,128)(2,1)}, bf16[1,512,384]{1,2,0:T(8,128)(2,1)}, u32[]{:S(2)}, u32[]{:S(2)}) collective-permute-start(bf16[1,512,384]{1,2,0:T(8,128)(2,1)} %bitcast.102), channel_id=1, source_target_pairs={{4,0},{5,1},{6,2},{7,3},{12,8},{13,9},{14,10},{15,11},{20,16},{21,... | collective-permute-start | bytes 1179656 | tf_op jit(solution)/shard_map/ppermute | solution.py:52
  619.0 44.1 %collective-permute-start.6 = (bf16[1,512,384]{1,2,0:T(8,128)(2,1)}, bf16[1,512,384]{1,2,0:T(8,128)(2,1)}, u32[]{:S(2)}, u32[]{:S(2)}) collective-permute-start(bf16[1,512,384]{1,2,0:T(8,128)(2,1)} %bitcast.92), channel_id=1, source_target_pairs={{4,0},{5,1},{6,2},{7,3},{12,8},{13,9},{14,10},{15,11},{20,16},{21,... | collective-permute-start | bytes 1179656 | tf_op jit(solution)/shard_map/ppermute | solution.py:52
  628.1 5.2 copy-start.24
  628.1 6.1 copy-start.35
  628.1 6.1 copy-start.39
  628.1 6.1 collective-permute-start.8
  662.7 96.6 %reduce-scatter.28.cloned.1.call-start = ((), (), s32[]{:S(2)}) async-start(), calls=%async_computation.24 | async-start | bytes 163840
  667.7 4.7 copy-start.27
  667.7 4.7 copy-start.29
  673.9 4.3 copy-start.67
  678.2 90.0 %reduce-scatter.26.cloned.1.call-start = ((), (), s32[]{:S(2)}) async-start(), calls=%async_computation.23 | async-start | bytes 3538944 | tf_op jit(solution)/shard_map/reduce_scatter | solution.py:339
  684.7 123.6 %reduce-scatter.20.cloned.1.call-start = ((), (), s32[]{:S(2)}) async-start(), calls=%async_computation.20 | async-start | bytes 1327104 | tf_op jit(solution)/shard_map/reduce_scatter | solution.py:330
  688.4 160.0 %reduce-scatter.22.cloned.1.call-start = ((), (), s32[]{:S(2)}) async-start(), calls=%async_computation.21 | async-start | bytes 1327104 | tf_op jit(solution)/shard_map/reduce_scatter | solution.py:333
  690.6 195.9 %reduce-scatter.16.cloned.1.call-start = ((), (), s32[]{:S(2)}) async-start(), calls=%async_computation.18 | async-start | bytes 1966080 | tf_op jit(solution)/shard_map/reduce_scatter | solution.py:308
  691.2 245.8 %reduce-scatter.18.cloned.1.call-start = ((), (), s32[]{:S(2)}) async-start(), calls=%async_computation.19 | async-start | bytes 3981312 | tf_op jit(solution)/shard_map/reduce_scatter | solution.py:324
  697.4 304.5 %reduce-scatter.24.cloned.1.call-start = ((), (), s32[]{:S(2)}) async-start(), calls=%async_computation.22 | async-start | bytes 7077888 | tf_op jit(solution)/shard_map/reduce_scatter | solution.py:336
  713.4 4.6 copy-start.57
  713.4 4.7 copy-start.68
  (54 other events, 121.8 us)
Sparse Core Ops, SparseCore 0:
  9.9 36.6 all-gather.7
  48.5 24.0 all-gather.9
  74.5 24.0 all-gather.11
  127.4 119.9 all-reduce.4
  249.6 44.5 all-gather.13
  295.6 37.0 all-gather.17
  334.6 31.1 all-gather.15
  381.3 121.0 all-reduce.6
  504.7 34.2 reduce-scatter.13
  662.8 35.1 reduce-scatter.29
  700.8 19.2 reduce-scatter.27
  723.7 44.4 reduce-scatter.25
  771.4 36.7 reduce-scatter.19
  811.7 36.7 reduce-scatter.21
  851.2 35.2 reduce-scatter.15
  889.9 47.0 reduce-scatter.17
  940.2 61.7 reduce-scatter.23
